TPU v7x, 256 devices: a whole 4x4x8 slice. The times are simulated.
256 devices in a mesh: tile: 32 (over x, z), ens: 8 (over y, core).
Axes of the slice: x: 4, y: 4, z: 8, core: 2. Of those that a mesh axis runs over, the one named last changes fastest.
Arguments:
- initial_sample_set: float32 [80, 2, 128, 2048], P('ens', None, 'tile'), may hold values from -6 to 6
- flow_velocity: float32 [2, 2, 128, 2048], P(None, None, 'tile'), may hold values from -0.4 to 0.4
- obs_loc: int32 [3, 2, 32768], P(None, None, 'tile'), may hold values from 0 to 2047, as said below
- obs_count: int32 [2, 32], P(None, 'tile'), may hold values from 256 to 1024, as said below
- obs_value: float32 [2, 32768], P(None, 'tile'), may hold values from -6 to 6
- obs_error: float32 [2, 32768], P(None, 'tile'), may hold values from 0.25 to 2
Outputs:
- analysis: float32 [80, 2, 128, 2048], P('ens', None, 'tile')
Inputs may be any that keep to these rules, and one draw needn't show every extreme that they name: `obs_loc`: slots 1024 * t to 1024 * (t + 1) - 1 of a batch belong to tile t: their row lies in rows 4 * t to 4 * (t + 1) - 1; columns lie in 0 to 2047 and levels in 0 to 1. `obs_count`: in every batch some tile has exactly 1024 live observations; a tile's live observations are its first slots.
All inputs are finite; a program needn't handle non-finite values.
Results may differ from a plain program's by a relative error of at most 0.0003.
Values sent between devices are 32-bit elements; how exact they have to be, the bound alone decides.
A program may use at most 128 MiB of HBM per device.

v0:
```python
import jax
import jax.numpy as jnp
from jax import lax
from jax.sharding import PartitionSpec as P

BATCHES = 2
REACH = 2
SPREAD_RATE = 0.05
EPSILON = 1e-06
PRECISE = lax.Precision.HIGHEST


def with_halo(cells, sides, width):
    for axis, dim in sides:
        count = lax.axis_size(axis)
        ends = count - 1
        head = lax.slice_in_dim(cells, 0, width, axis=dim)
        tail = lax.slice_in_dim(cells, cells.shape[dim] - width, cells.shape[dim], axis=dim)
        cells = jnp.concatenate(
            [
                lax.ppermute(tail, axis, [(i, (i + 1) % count) for i in range(ends)]),
                cells,
                lax.ppermute(head, axis, [((i + 1) % count, i) for i in range(ends)]),
            ],
            axis=dim,
        )
    return cells


def shifted(value, axis, steps):
    count = lax.axis_size(axis)
    leading, last = (max(0, -steps), min(count, count - steps))
    return lax.ppermute(value, axis, [(source, source + steps) for source in range(leading, last)])


def advance(centre, row_above, row_below, col_left, col_right, flow_velocity):
    wind_rows = flow_velocity[0][None]
    wind_cols = flow_velocity[1][None]
    tendency = (
        jnp.maximum(wind_rows, 0.0) * (centre - row_above)
        + jnp.minimum(wind_rows, 0.0) * (row_below - centre)
        + jnp.maximum(wind_cols, 0.0) * (centre - col_left)
        + jnp.minimum(wind_cols, 0.0) * (col_right - centre)
    )
    return (
        centre
        - tendency
        + SPREAD_RATE * (row_above + row_below + col_left + col_right - 4.0 * centre)
    )


def increments(prior_obs, row_values, error_row, live_mask):
    members = prior_obs.shape[0]
    average = jnp.sum(prior_obs, axis=0) / members
    deviation = prior_obs - average[None, :]
    var_prior = jnp.sum(deviation * deviation, axis=0) / (members - 1) + EPSILON
    combined = var_prior + error_row
    shrink_factor = jnp.sqrt(error_row / combined)
    mean_post = (error_row * average + var_prior * row_values) / combined
    obs_shift = live_mask[None, :] * (
        (shrink_factor - 1.0)[None, :] * deviation + (mean_post - average)[None, :]
    )
    weight = live_mask[None, :] * deviation / ((members - 1) * var_prior)[None, :]
    return (weight, obs_shift)


def block_gain(
    states, weight, obs_shift, obs_place, cell_lev, cell_row, cell_col, radius, col_radius
):
    covariance = lax.dot_general(
        weight,
        states,
        (((0,), (0,)), ((), ())),
        precision=PRECISE,
        preferred_element_type=jnp.float32,
    )
    row_gap = cell_row[None, :] - obs_place[0][:, None]
    column_spacing = cell_col[None, :] - obs_place[1][:, None]
    level_gap = jnp.abs(cell_lev[None, :] - obs_place[2][:, None])
    closeness = jnp.maximum(
        1.0
        - row_gap * row_gap / (radius * radius)
        - column_spacing * column_spacing / (col_radius * col_radius),
        0.0,
    )
    gain_map = covariance * (closeness * closeness / (1.0 + level_gap))
    return jnp.dot(obs_shift, gain_map, precision=PRECISE, preferred_element_type=jnp.float32)


def propagate_model(initial_sample_set, flow_velocity):
    padded = with_halo(initial_sample_set, (("tile", 2),), 1)
    padded = jnp.pad(padded, ((0, 0), (0, 0), (0, 0), (1, 1)))
    return advance(
        padded[:, :, 1:-1, 1:-1],
        padded[:, :, :-2, 1:-1],
        padded[:, :, 2:, 1:-1],
        padded[:, :, 1:-1, :-2],
        padded[:, :, 1:-1, 2:],
        flow_velocity,
    )


def analyse(
    columns,
    prior_obs,
    obs_place,
    row_values,
    error_row,
    live_mask,
    cell_lev,
    cell_row,
    cell_col,
    radius,
    col_radius,
):
    weight, obs_shift = increments(prior_obs, row_values, error_row, live_mask)
    payload = (weight, obs_shift, obs_place)
    received = [payload]
    for displacement in range(1, REACH + 1):
        received.append(shifted((payload[0], payload[1], payload[2]), "tile", displacement))
        received.append(shifted((payload[0], payload[1], payload[2]), "tile", -displacement))
    members = columns.shape[0]
    flat_state = columns.reshape(members, -1)
    increment = jnp.zeros_like(flat_state)
    for incoming in received:
        increment = increment + block_gain(
            flat_state,
            incoming[0],
            incoming[1],
            incoming[2],
            cell_lev,
            cell_row,
            cell_col,
            radius,
            col_radius,
        )
    return columns + increment.reshape(columns.shape)


def on_device(initial_sample_set, flow_velocity, obs_loc, obs_count, obs_value, obs_error):
    member_deviation, levels, row_count, col_total = initial_sample_set.shape
    ens_size = lax.axis_size("ens")
    col_count = col_total // ens_size
    obs_tile = obs_value.shape[1]
    tile_index = lax.axis_index("tile")
    ens_index = lax.axis_index("ens")
    radius = float(REACH * row_count)
    col_radius = float(col_total // 2)
    current_model_vector = propagate_model(initial_sample_set, flow_velocity)
    slots = jnp.arange(obs_tile, dtype=jnp.int32)
    cell_index = jnp.arange(levels * row_count * col_count, dtype=jnp.int32)
    cell_lev = (cell_index // (row_count * col_count)).astype(jnp.float32)
    cell_row = (tile_index * row_count + cell_index // col_count % row_count).astype(jnp.float32)
    cell_col = (ens_index * col_count + cell_index % col_count).astype(jnp.float32)
    for batch_index in range(BATCHES):
        local_row = obs_loc[0, batch_index] - tile_index * row_count
        flat_index = (obs_loc[2, batch_index] * row_count + local_row) * col_total + obs_loc[
            1, batch_index
        ]
        own_prior = jnp.take(current_model_vector.reshape(member_deviation, -1), flat_index, axis=1)
        prior_obs = lax.all_gather(own_prior, "ens", axis=0, tiled=True)
        columns = lax.all_to_all(
            current_model_vector, "ens", split_axis=3, concat_axis=0, tiled=True
        )
        live_mask = (slots < obs_count[batch_index, 0]).astype(jnp.float32)
        obs_place = obs_loc[:, batch_index].astype(jnp.float32)
        columns = analyse(
            columns,
            prior_obs,
            obs_place,
            obs_value[batch_index],
            obs_error[batch_index],
            live_mask,
            cell_lev,
            cell_row,
            cell_col,
            radius,
            col_radius,
        )
        current_model_vector = lax.all_to_all(
            columns, "ens", split_axis=0, concat_axis=3, tiled=True
        )
    return current_model_vector


def solution(mesh):
    in_specs = (
        P("ens", None, "tile", None),
        P(None, None, "tile", None),
        P(None, None, "tile"),
        P(None, "tile"),
        P(None, "tile"),
        P(None, "tile"),
    )
    out_specs = P("ens", None, "tile", None)
    return jax.shard_map(
        on_device, mesh=mesh, in_specs=in_specs, out_specs=out_specs, check_vma=False
    )
```

profile of v0, /device:TPU:2, one launch (start us, length us, event | category | flops | bytes accessed | tf_op | source)
XLA Modules:
  0.0 487.8 jit_solution(17337714978346496619)
XLA Ops:
  0.9 8.2 %collective-permute-start.13 = (f32[3,1024]{1,0:T(4,128)S(1)}, f32[3,1024]{1,0:T(4,128)S(1)}, u32[]{:S(2)}, u32[]{:S(2)}) collective-permute-start(f32[3,1024]{1,0:T(4,128)S(1)} %bitcast.143), channel_id=1, source_target_pairs={{16,0},{24,8},{32,16},{40,24},{48,32},{56,40},{64,48},{72,56},{80,... | collective-permute-start | bytes 36872 | tf_op jit(solution)/shard_map/ppermute | solution.py:33
  11.0 6.5 %collective-permute-start.7 = (f32[3,1024]{1,0:T(4,128)S(1)}, f32[3,1024]{1,0:T(4,128)S(1)}, u32[]{:S(2)}, u32[]{:S(2)}) collective-permute-start(f32[3,1024]{1,0:T(4,128)S(1)} %bitcast.145), channel_id=1, source_target_pairs={{8,0},{16,8},{24,16},{32,24},{40,32},{48,40},{56,48},{64,56},{72,6... | collective-permute-start | bytes 36872 | tf_op jit(solution)/shard_map/ppermute | solution.py:33
  19.4 4.4 collective-permute-start.25
  30.1 2.4 collective-permute-start.22
  32.5 8.1 %collective-permute-start.19 = (f32[3,1024]{1,0:T(4,128)S(1)}, f32[3,1024]{1,0:T(4,128)S(1)}, u32[]{:S(2)}, u32[]{:S(2)}) collective-permute-start(f32[3,1024]{1,0:T(4,128)S(1)} %bitcast.141), channel_id=1, source_target_pairs={{8,0},{16,8},{24,16},{32,24},{40,32},{48,40},{56,48},{64,56},{72,6... | collective-permute-start | bytes 36872 | tf_op jit(solution)/shard_map/ppermute | solution.py:33
  42.6 6.0 %collective-permute-start.1 = (f32[10,2,1,2048]{3,0,2,1:T(8,128)S(1)}, f32[10,2,1,2048]{3,0,2,1:T(8,128)S(1)}, u32[]{:S(2)}, u32[]{:S(2)}) collective-permute-start(f32[10,2,1,2048]{3,0,2,1:T(8,128)S(1)} %copy.150), channel_id=1, source_target_pairs={{8,0},{16,8},{24,16},{32,24},{40,32},{48,40},{56,48},{64,56},{72,6... | collective-permute-start | bytes 491528 | tf_op jit(solution)/shard_map/ppermute | solution.py:23
  52.7 6.4 %collective-permute-done = f32[10,2,1,2048]{3,0,2,1:T(8,128)S(1)} collective-permute-done((f32[10,2,1,2048]{3,0,2,1:T(8,128)S(1)}, f32[10,2,1,2048]{3,0,2,1:T(8,128)S(1)}, u32[]{:S(2)}, u32[]{:S(2)}) %collective-permute-start) | collective-permute-done | bytes 163872 | tf_op jit(solution)/shard_map/ppermute | solution.py:21
  59.3 2.3 select_maximum_fusion
  61.6 3.2 fusion.291
  64.8 4.7 copy.145
  69.5 5.9 %copy.134 = f32[10,2,4,2048]{0,2,1,3:T(4,128)} copy(f32[10,2,4,2048]{3,2,1,0:T(4,128)S(1)} %fusion.291) | data formatting | bytes 1310720 | tf_op jit(solution)/shard_map/add | solution.py:46
  75.5 6.2 %gather_fusion = f32[1024,10]{1,0:T(8,128)S(1)} fusion(f32[10,16384]{0,1:T(8,128)} %bitcast.124, s32[1024]{0:T(1024)S(1)} %fusion.316), kind=kCustom, calls=%fused_computation.clone | custom fusion | bytes 86016 | tf_op jit(solution)/shard_map/jit(_take)/gather | solution.py:160
  82.1 13.6 %all-gather = f32[8,10,1024]{2,1,0:T(8,128)S(1)} all-gather(f32[1,10,1024]{2,1,0:T(8,128)S(1)} %copy.137), channel_id=1, replica_groups=mesh['tile'=32,'ens'=8] {'ens'}, dimensions={0}, use_global_device_ids=true | all-gather | bytes 368640 | tf_op jit(solution)/shard_map/all_gather | solution.py:161
  95.8 12.3 %reshape.233 = f32[8,1,20480]{2,1,0:T(1,128)} reshape(f32[2048,2,4,10]{3,2,1,0:T(4,128)} %bitcast.120) | data formatting | bytes 1310720
  108.1 3.8 all-to-all-start
  114.0 2.1 collective-permute-start.12
  116.1 7.4 %all-to-all-done = f32[8,1,20480]{2,1,0:T(1,128)S(1)} async-done(((f32[8,1,20480]{2,1,0:T(1,128)}), f32[8,1,20480]{2,1,0:T(1,128)S(1)}, u32[]{:S(2)}, u32[]{:S(2)}) %all-to-all-start) | async-done | bytes 655392 | tf_op jit(solution)/shard_map/all_to_all | solution.py:162
  124.1 2.2 reduce.2
  126.3 14.6 %reshape.234 = f32[2048,2,4,10]{3,2,1,0:T(4,128)} reshape(f32[8,20480]{1,0:T(8,128)S(1)} %reduce.2) | data formatting | bytes 1310720
  140.9 7.2 %copy.135 = f32[10,2,4,8,256]{4,2,1,0,3:T(4,128)S(1)} copy(f32[10,2,4,8,256]{0,2,1,4,3:T(4,128)} %bitcast.121) | data formatting | bytes 1310720 | tf_op jit(solution)/shard_map/all_to_all | solution.py:162
  148.5 6.9 %fusion.370 = f32[1024,2048]{1,0:T(8,128)S(1)} fusion(f32[80,1024]{1,0:T(8,128)S(1)} %get-tuple-element.10, f32[80,2048]{1,0:T(8,128)S(1)} %reshape.202), kind=kOutput, calls=%fused_computation.408 | convolution fusion | flops 2013265920 | bytes 9371648 | tf_op jit(solution)/shard_map/dot_general | solution.py:70
  155.4 9.7 %fusion.144 = f32[80,2048]{1,0:T(8,128)S(1)} fusion(f32[80,1024]{1,0:T(8,128)S(1)} %get-tuple-element.11, f32[1024,2048]{1,0:T(8,128)S(1)} %fusion.370, f32[1024]{0:T(1024)S(1)} %bitcast.153, f32[2048]{0:T(1024)S(1)} %get-tuple-element.64, f32[1024]{0:T(1024)S(1)} %bitcast.152, f32[2048]{0:T(1024)S(1)} %fusion.311, f32[1024]{0:T(1024)S(1)} %bitcast.154, ...), kind=kOutput, calls=%fused_computation.146 | convolution fusion | flops 2044723200 | bytes 9408512 | tf_op jit(solution)/shard_map/dot_general | solution.py:87
  167.1 6.9 %fusion.374 = f32[1024,2048]{1,0:T(8,128)S(1)} fusion(f32[80,1024]{1,0:T(8,128)S(1)} %collective-permute-done.12, f32[80,2048]{1,0:T(8,128)S(1)} %reshape.202), kind=kOutput, calls=%fused_computation.412 | convolution fusion | flops 2013265920 | bytes 9371648 | tf_op jit(solution)/shard_map/dot_general | solution.py:70
  174.1 2.1 collective-permute-start.9
  176.2 9.6 %fusion.80 = f32[80,2048]{1,0:T(8,128)S(1)} fusion(f32[80,1024]{1,0:T(8,128)S(1)} %collective-permute-done.11, f32[1024,2048]{1,0:T(8,128)S(1)} %fusion.374, f32[1024]{0:T(1024)S(1)} %bitcast.171, f32[1024]{0:T(1024)S(1)} %bitcast.172, f32[1024]{0:T(1024)S(1)} %bitcast.170, f32[2048]{0:T(1024)S(1)} %get-tuple-element.64, f32[2048]{0:T(1024)S(1)} %fusion.311, ...), kind=kOutput, calls=%fused_computation.82 | convolution fusion | flops 2044723200 | bytes 9408512 | tf_op jit(solution)/shard_map/dot_general | solution.py:87
  185.8 13.4 %collective-permute-done.9 = f32[80,1024]{1,0:T(8,128)S(1)} collective-permute-done((f32[80,1024]{1,0:T(8,128)S(1)}, f32[80,1024]{1,0:T(8,128)S(1)}, u32[]{:S(2)}, u32[]{:S(2)}) %collective-permute-start.9) | collective-permute-done | bytes 327712 | tf_op jit(solution)/shard_map/ppermute | solution.py:33
  199.2 2.2 collective-permute-start.5
  201.4 6.9 %fusion.373 = f32[1024,2048]{1,0:T(8,128)S(1)} fusion(f32[80,1024]{1,0:T(8,128)S(1)} %collective-permute-done.9, f32[80,2048]{1,0:T(8,128)S(1)} %reshape.202), kind=kOutput, calls=%fused_computation.411 | convolution fusion | flops 2013265920 | bytes 9371648 | tf_op jit(solution)/shard_map/dot_general | solution.py:70
  208.3 2.5 collective-permute-start.6
  210.8 9.6 %fusion.96 = f32[80,2048]{1,0:T(8,128)S(1)} fusion(f32[80,1024]{1,0:T(8,128)S(1)} %collective-permute-done.8, f32[1024,2048]{1,0:T(8,128)S(1)} %fusion.373, f32[1024]{0:T(1024)S(1)} %bitcast.165, f32[1024]{0:T(1024)S(1)} %bitcast.166, f32[1024]{0:T(1024)S(1)} %bitcast.164, f32[2048]{0:T(1024)S(1)} %get-tuple-element.64, f32[2048]{0:T(1024)S(1)} %fusion.311, ...), kind=kOutput, calls=%fused_computation.98 | convolution fusion | flops 2044723200 | bytes 9408512 | tf_op jit(solution)/shard_map/dot_general | solution.py:87
  220.4 4.0 collective-permute-start.2
  224.4 6.9 %fusion.372 = f32[1024,2048]{1,0:T(8,128)S(1)} fusion(f32[80,1024]{1,0:T(8,128)S(1)} %collective-permute-done.6, f32[80,2048]{1,0:T(8,128)S(1)} %reshape.202), kind=kOutput, calls=%fused_computation.410 | convolution fusion | flops 2013265920 | bytes 9371648 | tf_op jit(solution)/shard_map/dot_general | solution.py:70
  231.3 4.1 collective-permute-start.3
  235.5 9.6 %fusion.112 = f32[80,2048]{1,0:T(8,128)S(1)} fusion(f32[80,1024]{1,0:T(8,128)S(1)} %collective-permute-done.5, f32[1024,2048]{1,0:T(8,128)S(1)} %fusion.372, f32[1024]{0:T(1024)S(1)} %bitcast.162, f32[1024]{0:T(1024)S(1)} %bitcast.163, f32[1024]{0:T(1024)S(1)} %bitcast.161, f32[2048]{0:T(1024)S(1)} %get-tuple-element.64, f32[2048]{0:T(1024)S(1)} %fusion.311, ...), kind=kOutput, calls=%fused_computation.114 | convolution fusion | flops 2044723200 | bytes 9408512 | tf_op jit(solution)/shard_map/dot_general | solution.py:87
  245.0 7.3 %fusion.371 = f32[1024,2048]{1,0:T(8,128)S(1)} fusion(f32[80,1024]{1,0:T(8,128)S(1)} %collective-permute-done.3, f32[80,2048]{1,0:T(8,128)S(1)} %reshape.202), kind=kOutput, calls=%fused_computation.409 | convolution fusion | flops 2013265920 | bytes 9371648 | tf_op jit(solution)/shard_map/dot_general | solution.py:70
  252.4 9.8 %fusion.269 = f32[80,2048]{1,0:T(8,128)S(1)} fusion(f32[80,2048]{1,0:T(8,128)S(1)} %fusion.80, f32[80,2048]{1,0:T(8,128)S(1)} %fusion.96, f32[80,2048]{1,0:T(8,128)S(1)} %fusion.112, f32[80,2048]{1,0:T(8,128)S(1)} %fusion.144, f32[80,1024]{1,0:T(8,128)S(1)} %collective-permute-done.2, f32[1024,2048]{1,0:T(8,128)S(1)} %fusion.371, f32[1024]{0:T(1024)S(1)} %bitcast.159, ...), kind=kOutput, calls=%fused_computation.265 | convolution fusion | flops 2045378560 | bytes 12029952 | tf_op jit(solution)/shard_map/dot_general | solution.py:87
  263.7 3.5 all-to-all-start.1
  267.3 11.6 %all-to-all-done.1 = f32[80,2,4,256]{3,2,1,0:T(4,128)S(1)} async-done(((f32[80,2,4,256]{3,2,1,0:T(4,128)}), f32[80,2,4,256]{3,2,1,0:T(4,128)S(1)}, u32[]{:S(2)}, u32[]{:S(2)}) %all-to-all-start.1) | async-done | bytes 655392 | tf_op jit(solution)/shard_map/all_to_all | solution.py:180
  278.9 4.7 copy.138
  283.6 6.2 %gather_fusion.1 = f32[1024,10]{1,0:T(8,128)S(1)} fusion(f32[10,16384]{0,1:T(8,128)} %bitcast.118, s32[1024]{0:T(1024)S(1)} %fusion.317), kind=kCustom, calls=%fused_computation.1.clone | custom fusion | bytes 86016 | tf_op jit(solution)/shard_map/jit(_take)/gather | solution.py:160
  290.2 13.1 %all-gather.1 = f32[8,10,1024]{2,1,0:T(8,128)S(1)} all-gather(f32[1,10,1024]{2,1,0:T(8,128)S(1)} %copy.142), channel_id=1, replica_groups=mesh['tile'=32,'ens'=8] {'ens'}, dimensions={0}, use_global_device_ids=true | all-gather | bytes 368640 | tf_op jit(solution)/shard_map/all_gather | solution.py:161
  303.4 12.0 %copy.139 = f32[10,2,4,8,256]{0,2,1,4,3:T(4,128)} copy(f32[10,2,4,8,256]{0,4,3,2,1:T(8,128)} %bitcast.119) | data formatting | bytes 1310720 | tf_op jit(solution)/shard_map/all_to_all | solution.py:180
  315.4 12.2 %reshape.235 = f32[8,1,20480]{2,1,0:T(1,128)} reshape(f32[2048,2,4,10]{3,2,1,0:T(4,128)} %bitcast.122) | data formatting | bytes 1310720
  327.7 3.5 all-to-all-start.2
  331.4 3.6 collective-permute-start.23
  335.0 3.2 collective-permute-start.20
  338.2 5.7 %collective-permute-start.24 = (f32[80,1024]{1,0:T(8,128)S(1)}, f32[80,1024]{1,0:T(8,128)S(1)}, u32[]{:S(2)}, u32[]{:S(2)}) collective-permute-start(f32[80,1024]{1,0:T(8,128)S(1)} %get-tuple-element.8), channel_id=1, source_target_pairs={{16,0},{24,8},{32,16},{40,24},{48,32},{56,40},{64,48},{72,56},{80,... | collective-permute-start | bytes 983048 | tf_op jit(solution)/shard_map/ppermute | solution.py:33
  345.8 7.6 %collective-permute-start.17 = (f32[80,1024]{1,0:T(8,128)S(1)}, f32[80,1024]{1,0:T(8,128)S(1)}, u32[]{:S(2)}, u32[]{:S(2)}) collective-permute-start(f32[80,1024]{1,0:T(8,128)S(1)} %get-tuple-element.9), channel_id=1, source_target_pairs={{8,0},{16,8},{24,16},{32,24},{40,32},{48,40},{56,48},{64,56},{72,6... | collective-permute-start | bytes 983048 | tf_op jit(solution)/shard_map/ppermute | solution.py:33
  353.4 2.2 reduce.3
  355.6 14.6 %reshape.236 = f32[2048,2,4,10]{3,2,1,0:T(4,128)} reshape(f32[8,20480]{1,0:T(8,128)S(1)} %reduce.3) | data formatting | bytes 1310720
  370.2 5.7 %copy.146 = f32[10,2,4,8,256]{4,3,2,1,0:T(8,128)S(1)} copy(f32[10,2,4,8,256]{0,2,1,4,3:T(4,128)} %bitcast.123) | data formatting | bytes 1310720 | tf_op jit(solution)/shard_map/all_to_all | solution.py:162
  376.5 6.9 %fusion.375 = f32[1024,2048]{1,0:T(8,128)S(1)} fusion(f32[80,1024]{1,0:T(8,128)S(1)} %get-tuple-element.8, f32[80,2048]{1,0:T(8,128)S(1)} %reshape.205), kind=kOutput, calls=%fused_computation.413 | convolution fusion | flops 2013265920 | bytes 9371648 | tf_op jit(solution)/shard_map/dot_general | solution.py:70
  383.4 9.7 %fusion.64 = f32[80,2048]{1,0:T(8,128)S(1)} fusion(f32[80,1024]{1,0:T(8,128)S(1)} %get-tuple-element.9, f32[1024,2048]{1,0:T(8,128)S(1)} %fusion.375, f32[1024]{0:T(1024)S(1)} %bitcast.150, f32[1024]{0:T(1024)S(1)} %bitcast.151, f32[1024]{0:T(1024)S(1)} %bitcast.149, f32[2048]{0:T(1024)S(1)} %get-tuple-element.64, f32[2048]{0:T(1024)S(1)} %fusion.311, ...), kind=kOutput, calls=%fused_computation.66 | convolution fusion | flops 2044723200 | bytes 9408512 | tf_op jit(solution)/shard_map/dot_general | solution.py:87
  395.2 6.9 %fusion.379 = f32[1024,2048]{1,0:T(8,128)S(1)} fusion(f32[80,1024]{1,0:T(8,128)S(1)} %collective-permute-done.24, f32[80,2048]{1,0:T(8,128)S(1)} %reshape.205), kind=kOutput, calls=%fused_computation.417 | convolution fusion | flops 2013265920 | bytes 9371648 | tf_op jit(solution)/shard_map/dot_general | solution.py:70
  402.2 4.1 collective-permute-start.14
  406.3 10.5 %fusion = f32[80,2048]{1,0:T(8,128)S(1)} fusion(f32[80,1024]{1,0:T(8,128)} %collective-permute-done.23, f32[1024,2048]{1,0:T(8,128)S(1)} %fusion.379, f32[1024]{0:T(1024)S(1)} %bitcast.156, f32[1024]{0:T(1024)S(1)} %bitcast.157, f32[1024]{0:T(1024)S(1)} %bitcast.155, f32[2048]{0:T(1024)S(1)} %get-tuple-element.64, f32[2048]{0:T(1024)S(1)} %fusion.311, ...), kind=kOutput, calls=%fused_computation.2 | convolution fusion | flops 2044723200 | bytes 9408512 | tf_op jit(solution)/shard_map/dot_general | solution.py:87
  416.8 2.3 collective-permute-start.15
  419.2 6.9 %fusion.378 = f32[1024,2048]{1,0:T(8,128)S(1)} fusion(f32[80,1024]{1,0:T(8,128)S(1)} %collective-permute-done.21, f32[80,2048]{1,0:T(8,128)S(1)} %reshape.205), kind=kOutput, calls=%fused_computation.416 | convolution fusion | flops 2013265920 | bytes 9371648 | tf_op jit(solution)/shard_map/dot_general | solution.py:70
  426.1 9.7 %fusion.16 = f32[80,2048]{1,0:T(8,128)S(1)} fusion(f32[80,1024]{1,0:T(8,128)S(1)} %collective-permute-done.20, f32[1024,2048]{1,0:T(8,128)S(1)} %fusion.378, f32[1024]{0:T(1024)S(1)} %bitcast.177, f32[1024]{0:T(1024)S(1)} %bitcast.178, f32[1024]{0:T(1024)S(1)} %bitcast.176, f32[2048]{0:T(1024)S(1)} %get-tuple-element.64, f32[2048]{0:T(1024)S(1)} %fusion.311, ...), kind=kOutput, calls=%fused_computation.18 | convolution fusion | flops 2044723200 | bytes 9408512 | tf_op jit(solution)/shard_map/dot_general | solution.py:87
  435.9 6.9 %fusion.377 = f32[1024,2048]{1,0:T(8,128)S(1)} fusion(f32[80,1024]{1,0:T(8,128)S(1)} %collective-permute-done.18, f32[80,2048]{1,0:T(8,128)S(1)} %reshape.205), kind=kOutput, calls=%fused_computation.415 | convolution fusion | flops 2013265920 | bytes 9371648 | tf_op jit(solution)/shard_map/dot_general | solution.py:70
  442.8 9.8 %fusion.32 = f32[80,2048]{1,0:T(8,128)S(1)} fusion(f32[80,1024]{1,0:T(8,128)S(1)} %collective-permute-done.17, f32[1024,2048]{1,0:T(8,128)S(1)} %fusion.377, f32[1024]{0:T(1024)S(1)} %bitcast.174, f32[1024]{0:T(1024)S(1)} %bitcast.175, f32[1024]{0:T(1024)S(1)} %bitcast.173, f32[2048]{0:T(1024)S(1)} %get-tuple-element.64, f32[2048]{0:T(1024)S(1)} %fusion.311, ...), kind=kOutput, calls=%fused_computation.34 | convolution fusion | flops 2044723200 | bytes 9408512 | tf_op jit(solution)/shard_map/dot_general | solution.py:87
  452.6 7.2 %fusion.376 = f32[1024,2048]{1,0:T(8,128)S(1)} fusion(f32[80,1024]{1,0:T(8,128)S(1)} %collective-permute-done.15, f32[80,2048]{1,0:T(8,128)S(1)} %reshape.205), kind=kOutput, calls=%fused_computation.414 | convolution fusion | flops 2013265920 | bytes 9371648 | tf_op jit(solution)/shard_map/dot_general | solution.py:70
  459.8 9.7 %fusion.281 = f32[80,2048]{1,0:T(8,128)S(1)} fusion(f32[80,2048]{1,0:T(8,128)S(1)} %fusion, f32[80,2048]{1,0:T(8,128)S(1)} %fusion.16, f32[80,2048]{1,0:T(8,128)S(1)} %fusion.32, f32[80,2048]{1,0:T(8,128)S(1)} %fusion.64, f32[80,1024]{1,0:T(8,128)S(1)} %collective-permute-done.14, f32[1024,2048]{1,0:T(8,128)S(1)} %fusion.376, f32[1024]{0:T(1024)S(1)} %bitcast.168, ...), kind=kOutput, calls=%fused_computation.269 | convolution fusion | flops 2045378560 | bytes 12029952 | tf_op jit(solution)/shard_map/dot_general | solution.py:87
  470.1 16.3 %all_to_all.72 = f32[80,2,4,256]{3,2,1,0:T(4,128)S(1)} all-to-all(f32[80,2,4,256]{3,2,1,0:T(4,128)S(1)} %bitcast_add_fusion.1), channel_id=1, replica_groups=mesh['tile'=32,'ens'=8] {'ens'}, dimensions={0} | all-to-all | bytes 1310720 | tf_op jit(solution)/shard_map/all_to_all | solution.py:180
  (98 shorter events, 30.8 us)
Async XLA Ops:
  0.9 29.2 %collective-permute-start.13 = (f32[3,1024]{1,0:T(4,128)S(1)}, f32[3,1024]{1,0:T(4,128)S(1)}, u32[]{:S(2)}, u32[]{:S(2)}) collective-permute-start(f32[3,1024]{1,0:T(4,128)S(1)} %bitcast.143), channel_id=1, source_target_pairs={{16,0},{24,8},{32,16},{40,24},{48,32},{56,40},{64,48},{72,56},{80,... | collective-permute-start | bytes 36872 | tf_op jit(solution)/shard_map/ppermute | solution.py:33
  9.0 23.5 %collective-permute-start.10 = (f32[3,1024]{1,0:T(4,128)S(1)}, f32[3,1024]{1,0:T(4,128)S(1)}, u32[]{:S(2)}, u32[]{:S(2)}) collective-permute-start(f32[3,1024]{1,0:T(4,128)S(1)} %bitcast.144), channel_id=1, source_target_pairs={{0,16},{8,24},{16,32},{24,40},{32,48},{40,56},{48,64},{56,72},{64,... | collective-permute-start | bytes 36872 | tf_op jit(solution)/shard_map/ppermute | solution.py:33
  11.0 29.7 %collective-permute-start.7 = (f32[3,1024]{1,0:T(4,128)S(1)}, f32[3,1024]{1,0:T(4,128)S(1)}, u32[]{:S(2)}, u32[]{:S(2)}) collective-permute-start(f32[3,1024]{1,0:T(4,128)S(1)} %bitcast.145), channel_id=1, source_target_pairs={{8,0},{16,8},{24,16},{32,24},{40,32},{48,40},{56,48},{64,56},{72,6... | collective-permute-start | bytes 36872 | tf_op jit(solution)/shard_map/ppermute | solution.py:33
  17.5 25.2 %collective-permute-start.4 = (f32[3,1024]{1,0:T(4,128)S(1)}, f32[3,1024]{1,0:T(4,128)S(1)}, u32[]{:S(2)}, u32[]{:S(2)}) collective-permute-start(f32[3,1024]{1,0:T(4,128)S(1)} %bitcast.146), channel_id=1, source_target_pairs={{0,8},{8,16},{16,24},{24,32},{32,40},{40,48},{48,56},{56,64},{64,7... | collective-permute-start | bytes 36872 | tf_op jit(solution)/shard_map/ppermute | solution.py:33
  19.4 29.3 %collective-permute-start.25 = (f32[3,1024]{1,0:T(4,128)S(1)}, f32[3,1024]{1,0:T(4,128)S(1)}, u32[]{:S(2)}, u32[]{:S(2)}) collective-permute-start(f32[3,1024]{1,0:T(4,128)S(1)} %bitcast.139), channel_id=1, source_target_pairs={{16,0},{24,8},{32,16},{40,24},{48,32},{56,40},{64,48},{72,56},{80,... | collective-permute-start | bytes 36872 | tf_op jit(solution)/shard_map/ppermute | solution.py:33
  30.1 237.2 %collective-permute-start.22 = (f32[3,1024]{1,0:T(4,128)S(1)}, f32[3,1024]{1,0:T(4,128)S(1)}, u32[]{:S(2)}, u32[]{:S(2)}) collective-permute-start(f32[3,1024]{1,0:T(4,128)S(1)} %bitcast.140), channel_id=1, source_target_pairs={{0,16},{8,24},{16,32},{24,40},{32,48},{40,56},{48,64},{56,72},{64,... | collective-permute-start | bytes 36872 | tf_op jit(solution)/shard_map/ppermute | solution.py:33
  32.5 234.8 %collective-permute-start.19 = (f32[3,1024]{1,0:T(4,128)S(1)}, f32[3,1024]{1,0:T(4,128)S(1)}, u32[]{:S(2)}, u32[]{:S(2)}) collective-permute-start(f32[3,1024]{1,0:T(4,128)S(1)} %bitcast.141), channel_id=1, source_target_pairs={{8,0},{16,8},{24,16},{32,24},{40,32},{48,40},{56,48},{64,56},{72,6... | collective-permute-start | bytes 36872 | tf_op jit(solution)/shard_map/ppermute | solution.py:33
  40.7 226.6 %collective-permute-start.16 = (f32[3,1024]{1,0:T(4,128)S(1)}, f32[3,1024]{1,0:T(4,128)S(1)}, u32[]{:S(2)}, u32[]{:S(2)}) collective-permute-start(f32[3,1024]{1,0:T(4,128)S(1)} %bitcast.142), channel_id=1, source_target_pairs={{0,8},{8,16},{16,24},{24,32},{32,40},{40,48},{48,56},{56,64},{64,7... | collective-permute-start | bytes 36872 | tf_op jit(solution)/shard_map/ppermute | solution.py:33
  42.6 9.9 %collective-permute-start.1 = (f32[10,2,1,2048]{3,0,2,1:T(8,128)S(1)}, f32[10,2,1,2048]{3,0,2,1:T(8,128)S(1)}, u32[]{:S(2)}, u32[]{:S(2)}) collective-permute-start(f32[10,2,1,2048]{3,0,2,1:T(8,128)S(1)} %copy.150), channel_id=1, source_target_pairs={{8,0},{16,8},{24,16},{32,24},{40,32},{48,40},{56,48},{64,56},{72,6... | collective-permute-start | bytes 491528 | tf_op jit(solution)/shard_map/ppermute | solution.py:23
  48.7 10.4 %collective-permute-start = (f32[10,2,1,2048]{3,0,2,1:T(8,128)S(1)}, f32[10,2,1,2048]{3,0,2,1:T(8,128)S(1)}, u32[]{:S(2)}, u32[]{:S(2)}) collective-permute-start(f32[10,2,1,2048]{3,0,2,1:T(8,128)S(1)} %copy.149), channel_id=1, source_target_pairs={{0,8},{8,16},{16,24},{24,32},{32,40},{40,48},{48,56},{56,64},{64,7... | collective-permute-start | bytes 491528 | tf_op jit(solution)/shard_map/ppermute | solution.py:21
  75.5 36.4 %copy-start = (f32[2,1024]{1,0:T(2,128)S(1)}, f32[2,1024]{1,0:T(2,128)}, u32[]{:S(2)}) copy-start(f32[2,1024]{1,0:T(2,128)} %param.13) | copy-start | bytes 24580
  75.5 36.5 %copy-start.1 = (f32[2,1024]{1,0:T(2,128)S(1)}, f32[2,1024]{1,0:T(2,128)}, u32[]{:S(2)}) copy-start(f32[2,1024]{1,0:T(2,128)} %param.12) | copy-start | bytes 24580
  108.1 15.5 %all-to-all-start = ((f32[8,1,20480]{2,1,0:T(1,128)}), f32[8,1,20480]{2,1,0:T(1,128)S(1)}, u32[]{:S(2)}, u32[]{:S(2)}) async-start(f32[8,1,20480]{2,1,0:T(1,128)} %reshape.233), calls=%async_computation | async-start | bytes 1310720 | tf_op jit(solution)/shard_map/all_to_all | solution.py:162
  112.1 62.0 %collective-permute-start.11 = (f32[80,1024]{1,0:T(8,128)S(1)}, f32[80,1024]{1,0:T(8,128)S(1)}, u32[]{:S(2)}, u32[]{:S(2)}) collective-permute-start(f32[80,1024]{1,0:T(8,128)S(1)} %get-tuple-element.11), channel_id=1, source_target_pairs={{16,0},{24,8},{32,16},{40,24},{48,32},{56,40},{64,48},{72,56},{80,... | collective-permute-start | bytes 983048 | tf_op jit(solution)/shard_map/ppermute | solution.py:33
  114.0 51.2 %collective-permute-start.12 = (f32[80,1024]{1,0:T(8,128)S(1)}, f32[80,1024]{1,0:T(8,128)S(1)}, u32[]{:S(2)}, u32[]{:S(2)}) collective-permute-start(f32[80,1024]{1,0:T(8,128)S(1)} %get-tuple-element.10), channel_id=1, source_target_pairs={{16,0},{24,8},{32,16},{40,24},{48,32},{56,40},{64,48},{72,56},{80,... | collective-permute-start | bytes 983048 | tf_op jit(solution)/shard_map/ppermute | solution.py:33
  165.2 43.2 %collective-permute-start.8 = (f32[80,1024]{1,0:T(8,128)S(1)}, f32[80,1024]{1,0:T(8,128)S(1)}, u32[]{:S(2)}, u32[]{:S(2)}) collective-permute-start(f32[80,1024]{1,0:T(8,128)S(1)} %get-tuple-element.11), channel_id=1, source_target_pairs={{0,16},{8,24},{16,32},{24,40},{32,48},{40,56},{48,64},{56,72},{64,... | collective-permute-start | bytes 983048 | tf_op jit(solution)/shard_map/ppermute | solution.py:33
  174.1 25.1 %collective-permute-start.9 = (f32[80,1024]{1,0:T(8,128)S(1)}, f32[80,1024]{1,0:T(8,128)S(1)}, u32[]{:S(2)}, u32[]{:S(2)}) collective-permute-start(f32[80,1024]{1,0:T(8,128)S(1)} %get-tuple-element.10), channel_id=1, source_target_pairs={{0,16},{8,24},{16,32},{24,40},{32,48},{40,56},{48,64},{56,72},{64,... | collective-permute-start | bytes 983048 | tf_op jit(solution)/shard_map/ppermute | solution.py:33
  199.2 32.1 %collective-permute-start.5 = (f32[80,1024]{1,0:T(8,128)S(1)}, f32[80,1024]{1,0:T(8,128)S(1)}, u32[]{:S(2)}, u32[]{:S(2)}) collective-permute-start(f32[80,1024]{1,0:T(8,128)S(1)} %get-tuple-element.11), channel_id=1, source_target_pairs={{8,0},{16,8},{24,16},{32,24},{40,32},{48,40},{56,48},{64,56},{72,6... | collective-permute-start | bytes 983048 | tf_op jit(solution)/shard_map/ppermute | solution.py:33
  208.3 12.0 %collective-permute-start.6 = (f32[80,1024]{1,0:T(8,128)S(1)}, f32[80,1024]{1,0:T(8,128)S(1)}, u32[]{:S(2)}, u32[]{:S(2)}) collective-permute-start(f32[80,1024]{1,0:T(8,128)S(1)} %get-tuple-element.10), channel_id=1, source_target_pairs={{8,0},{16,8},{24,16},{32,24},{40,32},{48,40},{56,48},{64,56},{72,6... | collective-permute-start | bytes 983048 | tf_op jit(solution)/shard_map/ppermute | solution.py:33
  220.4 32.0 %collective-permute-start.2 = (f32[80,1024]{1,0:T(8,128)S(1)}, f32[80,1024]{1,0:T(8,128)S(1)}, u32[]{:S(2)}, u32[]{:S(2)}) collective-permute-start(f32[80,1024]{1,0:T(8,128)S(1)} %get-tuple-element.11), channel_id=1, source_target_pairs={{0,8},{8,16},{16,24},{24,32},{32,40},{40,48},{48,56},{56,64},{64,7... | collective-permute-start | bytes 983048 | tf_op jit(solution)/shard_map/ppermute | solution.py:33
  231.3 13.7 %collective-permute-start.3 = (f32[80,1024]{1,0:T(8,128)S(1)}, f32[80,1024]{1,0:T(8,128)S(1)}, u32[]{:S(2)}, u32[]{:S(2)}) collective-permute-start(f32[80,1024]{1,0:T(8,128)S(1)} %get-tuple-element.10), channel_id=1, source_target_pairs={{0,8},{8,16},{16,24},{24,32},{32,40},{40,48},{48,56},{56,64},{64,7... | collective-permute-start | bytes 983048 | tf_op jit(solution)/shard_map/ppermute | solution.py:33
  263.7 15.2 %all-to-all-start.1 = ((f32[80,2,4,256]{3,2,1,0:T(4,128)}), f32[80,2,4,256]{3,2,1,0:T(4,128)S(1)}, u32[]{:S(2)}, u32[]{:S(2)}) async-start(f32[80,2,4,256]{3,2,1,0:T(4,128)} %bitcast_add_fusion), calls=%async_computation.1 | async-start | bytes 1310720 | tf_op jit(solution)/shard_map/all_to_all | solution.py:180
  327.7 25.8 %all-to-all-start.2 = ((f32[8,1,20480]{2,1,0:T(1,128)}), f32[8,1,20480]{2,1,0:T(1,128)S(1)}, u32[]{:S(2)}, u32[]{:S(2)}) async-start(f32[8,1,20480]{2,1,0:T(1,128)} %reshape.235), calls=%async_computation.2 | async-start | bytes 1310720 | tf_op jit(solution)/shard_map/all_to_all | solution.py:162
  331.4 70.8 %collective-permute-start.23 = (f32[80,1024]{1,0:T(8,128)S(1)}, f32[80,1024]{1,0:T(8,128)}, u32[]{:S(2)}, u32[]{:S(2)}) collective-permute-start(f32[80,1024]{1,0:T(8,128)S(1)} %get-tuple-element.9), channel_id=1, source_target_pairs={{16,0},{24,8},{32,16},{40,24},{48,32},{56,40},{64,48},{72,56},{80,... | collective-permute-start | bytes 983048 | tf_op jit(solution)/shard_map/ppermute | solution.py:33
  335.0 91.1 %collective-permute-start.20 = (f32[80,1024]{1,0:T(8,128)S(1)}, f32[80,1024]{1,0:T(8,128)S(1)}, u32[]{:S(2)}, u32[]{:S(2)}) collective-permute-start(f32[80,1024]{1,0:T(8,128)S(1)} %get-tuple-element.9), channel_id=1, source_target_pairs={{0,16},{8,24},{16,32},{24,40},{32,48},{40,56},{48,64},{56,72},{64,... | collective-permute-start | bytes 983048 | tf_op jit(solution)/shard_map/ppermute | solution.py:33
  338.2 55.0 %collective-permute-start.24 = (f32[80,1024]{1,0:T(8,128)S(1)}, f32[80,1024]{1,0:T(8,128)S(1)}, u32[]{:S(2)}, u32[]{:S(2)}) collective-permute-start(f32[80,1024]{1,0:T(8,128)S(1)} %get-tuple-element.8), channel_id=1, source_target_pairs={{16,0},{24,8},{32,16},{40,24},{48,32},{56,40},{64,48},{72,56},{80,... | collective-permute-start | bytes 983048 | tf_op jit(solution)/shard_map/ppermute | solution.py:33
  343.9 73.0 %collective-permute-start.21 = (f32[80,1024]{1,0:T(8,128)S(1)}, f32[80,1024]{1,0:T(8,128)S(1)}, u32[]{:S(2)}, u32[]{:S(2)}) collective-permute-start(f32[80,1024]{1,0:T(8,128)S(1)} %get-tuple-element.8), channel_id=1, source_target_pairs={{0,16},{8,24},{16,32},{24,40},{32,48},{40,56},{48,64},{56,72},{64,... | collective-permute-start | bytes 983048 | tf_op jit(solution)/shard_map/ppermute | solution.py:33
  345.8 97.0 %collective-permute-start.17 = (f32[80,1024]{1,0:T(8,128)S(1)}, f32[80,1024]{1,0:T(8,128)S(1)}, u32[]{:S(2)}, u32[]{:S(2)}) collective-permute-start(f32[80,1024]{1,0:T(8,128)S(1)} %get-tuple-element.9), channel_id=1, source_target_pairs={{8,0},{16,8},{24,16},{32,24},{40,32},{48,40},{56,48},{64,56},{72,6... | collective-permute-start | bytes 983048 | tf_op jit(solution)/shard_map/ppermute | solution.py:33
  393.2 13.1 %copy-start.2 = (f32[1,1024]{1,0:T(1,128)S(1)}, f32[1,1024]{1,0:T(1,128)}, u32[]{:S(2)}) copy-start(f32[1,1024]{1,0:T(1,128)} %get-tuple-element.29) | copy-start | bytes 12292
  393.2 13.1 %copy-start.3 = (f32[1,1024]{1,0:T(1,128)S(1)}, f32[1,1024]{1,0:T(1,128)}, u32[]{:S(2)}) copy-start(f32[1,1024]{1,0:T(1,128)} %get-tuple-element.30) | copy-start | bytes 12292
  393.2 13.1 %copy-start.4 = (f32[1,1024]{1,0:T(1,128)S(1)}, f32[1,1024]{1,0:T(1,128)}, u32[]{:S(2)}) copy-start(f32[1,1024]{1,0:T(1,128)} %get-tuple-element.31) | copy-start | bytes 12292
  393.2 42.6 %collective-permute-start.18 = (f32[80,1024]{1,0:T(8,128)S(1)}, f32[80,1024]{1,0:T(8,128)S(1)}, u32[]{:S(2)}, u32[]{:S(2)}) collective-permute-start(f32[80,1024]{1,0:T(8,128)S(1)} %get-tuple-element.8), channel_id=1, source_target_pairs={{8,0},{16,8},{24,16},{32,24},{40,32},{48,40},{56,48},{64,56},{72,6... | collective-permute-start | bytes 983048 | tf_op jit(solution)/shard_map/ppermute | solution.py:33
  402.2 57.6 %collective-permute-start.14 = (f32[80,1024]{1,0:T(8,128)S(1)}, f32[80,1024]{1,0:T(8,128)S(1)}, u32[]{:S(2)}, u32[]{:S(2)}) collective-permute-start(f32[80,1024]{1,0:T(8,128)S(1)} %get-tuple-element.9), channel_id=1, source_target_pairs={{0,8},{8,16},{16,24},{24,32},{32,40},{40,48},{48,56},{56,64},{64,7... | collective-permute-start | bytes 983048 | tf_op jit(solution)/shard_map/ppermute | solution.py:33
  416.8 35.8 %collective-permute-start.15 = (f32[80,1024]{1,0:T(8,128)S(1)}, f32[80,1024]{1,0:T(8,128)S(1)}, u32[]{:S(2)}, u32[]{:S(2)}) collective-permute-start(f32[80,1024]{1,0:T(8,128)S(1)} %get-tuple-element.8), channel_id=1, source_target_pairs={{0,8},{8,16},{16,24},{24,32},{32,40},{40,48},{48,56},{56,64},{64,7... | collective-permute-start | bytes 983048 | tf_op jit(solution)/shard_map/ppermute | solution.py:33
where the time goes:
time: 496 us; the launch traced here: 488 us
  matrix products  168 us (34%)
  local copies, waits for them, and re-layouts  114 us (23%)
  starting transfers between devices  105 us (21%)
  blocking collectives  43 us (9%)
  waiting for transfers between devices  40.2 us (8%)
  other arithmetic  15.9 us (3%)
    dot_general x10, matrix products, block_gain(): jnp.dot(obs_shift, gain_map, precision=PRECISE, preferred_element_type=jn...  97.6 us
    ppermute x24, starting transfers between devices, shifted(): lax.ppermute(value, axis, [(source, source + steps) for source in range(l...  86.5 us
    dot_general x10, matrix products, block_gain(): lax.dot_general(weight, states, (((0,), (0,)), ((), ())), precision=PRECI...  70 us
    unnamed x22, local copies, waits for them, and re-layouts  54.4 us
    all_gather x2, blocking collectives, on_device(): prior_obs = lax.all_gather(own_prior, 'ens', axis=0, tiled=True)  26.7 us
    all_to_all x3, local copies, waits for them, and re-layouts, on_device(): lax.all_to_all(columns, 'ens', split_axis=0, concat_axis=3, tiled=True)  17.7 us
    all_to_all x1, blocking collectives, on_device(): lax.all_to_all(columns, 'ens', split_axis=0, concat_axis=3, tiled=True)  16.3 us
    all_to_all x4, local copies, waits for them, and re-layouts, on_device(): lax.all_to_all(current_model_vector, 'ens', split_axis=3, concat_axis=0,...  13.7 us
  transfers between devices with their start and end apart: 29, of which 5 were waited for; matrix products, arithmetic and copies ran while one was open for 51% of the time, Pallas kernels for 0%

commit v1 on v0

--- a/solution.py
+++ b/solution.py
@@ -158,7 +158,9 @@
             1, batch_index
         ]
         own_prior = jnp.take(current_model_vector.reshape(member_deviation, -1), flat_index, axis=1)
-        prior_obs = lax.all_gather(own_prior, "ens", axis=0, tiled=True)
+        carry_in = jnp.stack(tuple((own_prior for _ in range(lax.axis_size("ens")))))
+        a_next = lax.all_to_all(carry_in, "ens", 0, 0)
+        prior_obs = jnp.concatenate(a_next, axis=0)
         columns = lax.all_to_all(
             current_model_vector, "ens", split_axis=3, concat_axis=0, tiled=True
         )

time: 496 us -> 493 us (level)
  the two profiles are of different devices: /device:TPU:2 before, /device:TPU:6 now
where the time goes in v1:
time: 493 us; the launch traced here: 485 us
  matrix products  169 us (34%)
  starting transfers between devices  117 us (24%)
  local copies, waits for them, and re-layouts  116 us (24%)
  waiting for transfers between devices  48.3 us (10%)
  blocking collectives  16.4 us (3%)
  other arithmetic  16.1 us (3%)
    dot_general x10, matrix products, block_gain(): jnp.dot(obs_shift, gain_map, precision=PRECISE, preferred_element_type=jn...  99.4 us
    ppermute x24, starting transfers between devices, shifted(): lax.ppermute(value, axis, [(source, source + steps) for source in range(l...  88 us
    dot_general x10, matrix products, block_gain(): lax.dot_general(weight, states, (((0,), (0,)), ((), ())), precision=PRECI...  69.6 us
    unnamed x14, local copies, waits for them, and re-layouts  54 us
    ppermute x24, waiting for transfers between devices, shifted(): lax.ppermute(value, axis, [(source, source + steps) for source in range(l...  28 us
    all_to_all x3, local copies, waits for them, and re-layouts, on_device(): lax.all_to_all(columns, 'ens', split_axis=0, concat_axis=3, tiled=True)  17.7 us
    all_to_all x1, blocking collectives, on_device(): lax.all_to_all(columns, 'ens', split_axis=0, concat_axis=3, tiled=True)  16.4 us
    all_to_all x4, local copies, waits for them, and re-layouts, on_device(): lax.all_to_all(current_model_vector, 'ens', split_axis=3, concat_axis=0,...  13.7 us
  transfers between devices with their start and end apart: 31, of which 8 were waited for; matrix products, arithmetic and copies ran while one was open for 60% of the time, Pallas kernels for 0%

profile of v1, /device:TPU:6, one launch (start us, length us, event | category | flops | bytes accessed | tf_op | source)
XLA Modules:
  0.0 484.6 jit_solution(8072913888124517805)
XLA Ops:
  0.9 8.5 %collective-permute-start.13 = (f32[3,1024]{1,0:T(4,128)S(1)}, f32[3,1024]{1,0:T(4,128)S(1)}, u32[]{:S(2)}, u32[]{:S(2)}) collective-permute-start(f32[3,1024]{1,0:T(4,128)S(1)} %bitcast.139), channel_id=1, source_target_pairs={{16,0},{24,8},{32,16},{40,24},{48,32},{56,40},{64,48},{72,56},{80,... | collective-permute-start | bytes 36872 | tf_op jit(solution)/shard_map/ppermute | solution.py:33
  11.3 6.5 %collective-permute-start.7 = (f32[3,1024]{1,0:T(4,128)S(1)}, f32[3,1024]{1,0:T(4,128)S(1)}, u32[]{:S(2)}, u32[]{:S(2)}) collective-permute-start(f32[3,1024]{1,0:T(4,128)S(1)} %bitcast.141), channel_id=1, source_target_pairs={{8,0},{16,8},{24,16},{32,24},{40,32},{48,40},{56,48},{64,56},{72,6... | collective-permute-start | bytes 36872 | tf_op jit(solution)/shard_map/ppermute | solution.py:33
  21.4 6.0 %collective-permute-start.1 = (f32[10,2,1,2048]{3,0,2,1:T(8,128)S(1)}, f32[10,2,1,2048]{3,0,2,1:T(8,128)S(1)}, u32[]{:S(2)}, u32[]{:S(2)}) collective-permute-start(f32[10,2,1,2048]{3,0,2,1:T(8,128)S(1)} %copy.152), channel_id=1, source_target_pairs={{8,0},{16,8},{24,16},{32,24},{40,32},{48,40},{56,48},{64,56},{72,6... | collective-permute-start | bytes 491528 | tf_op jit(solution)/shard_map/ppermute | solution.py:23
  33.3 3.4 collective-permute-start.25
  36.8 3.4 collective-permute-start.22
  42.0 6.4 %collective-permute-start.19 = (f32[3,1024]{1,0:T(4,128)S(1)}, f32[3,1024]{1,0:T(4,128)S(1)}, u32[]{:S(2)}, u32[]{:S(2)}) collective-permute-start(f32[3,1024]{1,0:T(4,128)S(1)} %bitcast.137), channel_id=1, source_target_pairs={{8,0},{16,8},{24,16},{32,24},{40,32},{48,40},{56,48},{64,56},{72,6... | collective-permute-start | bytes 36872 | tf_op jit(solution)/shard_map/ppermute | solution.py:33
  48.6 2.3 select_maximum_fusion
  51.0 3.2 fusion.291
  54.2 4.7 copy.147
  58.9 6.2 %gather_fusion = f32[1024,10]{1,0:T(8,128)S(1)} fusion(f32[10,16384]{0,1:T(8,128)} %bitcast.120, s32[1024]{0:T(1024)S(1)} %fusion.316), kind=kCustom, calls=%fused_computation.clone | custom fusion | bytes 86016 | tf_op jit(solution)/shard_map/jit(_take)/gather | solution.py:160
  66.4 4.5 all-to-all-start.1
  72.9 6.0 %copy.136 = f32[10,2,4,2048]{0,2,1,3:T(4,128)} copy(f32[10,2,4,2048]{3,2,1,0:T(4,128)S(1)} %fusion.291) | data formatting | bytes 1310720 | tf_op jit(solution)/shard_map/add | solution.py:46
  78.9 12.2 %reshape.283 = f32[8,1,20480]{2,1,0:T(1,128)} reshape(f32[2048,2,4,10]{3,2,1,0:T(4,128)} %bitcast.116) | data formatting | bytes 1310720
  91.2 4.8 all-to-all-start
  96.3 3.6 collective-permute-start.12
  100.1 7.6 %all-to-all-done = f32[8,1,20480]{2,1,0:T(1,128)S(1)} async-done(((f32[8,1,20480]{2,1,0:T(1,128)}), f32[8,1,20480]{2,1,0:T(1,128)S(1)}, u32[]{:S(2)}, u32[]{:S(2)}) %all-to-all-start) | async-done | bytes 655392 | tf_op jit(solution)/shard_map/all_to_all | solution.py:164
  110.5 14.6 %reshape.284 = f32[2048,2,4,10]{3,2,1,0:T(4,128)} reshape(f32[8,20480]{1,0:T(8,128)S(1)} %reduce.4) | data formatting | bytes 1310720
  125.1 7.2 %copy.137 = f32[10,2,4,8,256]{4,2,1,0,3:T(4,128)S(1)} copy(f32[10,2,4,8,256]{0,2,1,4,3:T(4,128)} %bitcast.117) | data formatting | bytes 1310720 | tf_op jit(solution)/shard_map/all_to_all | solution.py:164
  132.7 6.9 %fusion.370 = f32[1024,2048]{1,0:T(8,128)S(1)} fusion(f32[80,1024]{1,0:T(8,128)S(1)} %div.191, f32[80,2048]{1,0:T(8,128)S(1)} %reshape.255), kind=kOutput, calls=%fused_computation.410 | convolution fusion | flops 2013265920 | bytes 9371648 | tf_op jit(solution)/shard_map/dot_general | solution.py:70
  139.7 9.7 %fusion.144 = f32[80,2048]{1,0:T(8,128)S(1)} fusion(f32[80,1024]{1,0:T(8,128)S(1)} %get-tuple-element.11, f32[1024,2048]{1,0:T(8,128)S(1)} %fusion.370, f32[1024]{0:T(1024)S(1)} %bitcast.149, f32[2048]{0:T(1024)S(1)} %get-tuple-element.64, f32[1024]{0:T(1024)S(1)} %bitcast.148, f32[2048]{0:T(1024)S(1)} %fusion.311, f32[1024]{0:T(1024)S(1)} %bitcast.150, ...), kind=kOutput, calls=%fused_computation.146 | convolution fusion | flops 2044723200 | bytes 9408512 | tf_op jit(solution)/shard_map/dot_general | solution.py:87
  149.4 3.4 collective-permute-start.11
  152.8 6.9 %fusion.374 = f32[1024,2048]{1,0:T(8,128)S(1)} fusion(f32[80,1024]{1,0:T(8,128)S(1)} %collective-permute-done.12, f32[80,2048]{1,0:T(8,128)S(1)} %reshape.255), kind=kOutput, calls=%fused_computation.414 | convolution fusion | flops 2013265920 | bytes 9371648 | tf_op jit(solution)/shard_map/dot_general | solution.py:70
  159.7 7.0 %collective-permute-done.11 = f32[80,1024]{1,0:T(8,128)S(1)} collective-permute-done((f32[80,1024]{1,0:T(8,128)S(1)}, f32[80,1024]{1,0:T(8,128)S(1)}, u32[]{:S(2)}, u32[]{:S(2)}) %collective-permute-start.11) | collective-permute-done | bytes 327712 | tf_op jit(solution)/shard_map/ppermute | solution.py:33
  168.9 9.5 %fusion.80 = f32[80,2048]{1,0:T(8,128)S(1)} fusion(f32[80,1024]{1,0:T(8,128)S(1)} %collective-permute-done.11, f32[1024,2048]{1,0:T(8,128)S(1)} %fusion.374, f32[1024]{0:T(1024)S(1)} %bitcast.155, f32[1024]{0:T(1024)S(1)} %bitcast.156, f32[1024]{0:T(1024)S(1)} %bitcast.154, f32[2048]{0:T(1024)S(1)} %get-tuple-element.64, f32[2048]{0:T(1024)S(1)} %fusion.311, ...), kind=kOutput, calls=%fused_computation.82 | convolution fusion | flops 2044723200 | bytes 9408512 | tf_op jit(solution)/shard_map/dot_general | solution.py:87
  178.4 9.8 %collective-permute-done.9 = f32[80,1024]{1,0:T(8,128)S(1)} collective-permute-done((f32[80,1024]{1,0:T(8,128)S(1)}, f32[80,1024]{1,0:T(8,128)S(1)}, u32[]{:S(2)}, u32[]{:S(2)}) %collective-permute-start.9) | collective-permute-done | bytes 327712 | tf_op jit(solution)/shard_map/ppermute | solution.py:33
  190.4 6.9 %fusion.373 = f32[1024,2048]{1,0:T(8,128)S(1)} fusion(f32[80,1024]{1,0:T(8,128)S(1)} %collective-permute-done.9, f32[80,2048]{1,0:T(8,128)S(1)} %reshape.255), kind=kOutput, calls=%fused_computation.413 | convolution fusion | flops 2013265920 | bytes 9371648 | tf_op jit(solution)/shard_map/dot_general | solution.py:70
  197.3 9.9 %collective-permute-done.8 = f32[80,1024]{1,0:T(8,128)S(1)} collective-permute-done((f32[80,1024]{1,0:T(8,128)S(1)}, f32[80,1024]{1,0:T(8,128)S(1)}, u32[]{:S(2)}, u32[]{:S(2)}) %collective-permute-start.8) | collective-permute-done | bytes 327712 | tf_op jit(solution)/shard_map/ppermute | solution.py:33
  207.2 2.4 collective-permute-start.6
  209.6 9.5 %fusion.96 = f32[80,2048]{1,0:T(8,128)S(1)} fusion(f32[80,1024]{1,0:T(8,128)S(1)} %collective-permute-done.8, f32[1024,2048]{1,0:T(8,128)S(1)} %fusion.373, f32[1024]{0:T(1024)S(1)} %bitcast.152, f32[1024]{0:T(1024)S(1)} %bitcast.153, f32[1024]{0:T(1024)S(1)} %bitcast.151, f32[2048]{0:T(1024)S(1)} %get-tuple-element.64, f32[2048]{0:T(1024)S(1)} %fusion.311, ...), kind=kOutput, calls=%fused_computation.98 | convolution fusion | flops 2044723200 | bytes 9408512 | tf_op jit(solution)/shard_map/dot_general | solution.py:87
  219.2 2.7 collective-permute-start.5
  221.9 6.9 %fusion.372 = f32[1024,2048]{1,0:T(8,128)S(1)} fusion(f32[80,1024]{1,0:T(8,128)S(1)} %collective-permute-done.6, f32[80,2048]{1,0:T(8,128)S(1)} %reshape.255), kind=kOutput, calls=%fused_computation.412 | convolution fusion | flops 2013265920 | bytes 9371648 | tf_op jit(solution)/shard_map/dot_general | solution.py:70
  229.3 3.8 collective-permute-start.3
  233.2 9.5 %fusion.112 = f32[80,2048]{1,0:T(8,128)S(1)} fusion(f32[80,1024]{1,0:T(8,128)S(1)} %collective-permute-done.5, f32[1024,2048]{1,0:T(8,128)S(1)} %fusion.372, f32[1024]{0:T(1024)S(1)} %bitcast.173, f32[1024]{0:T(1024)S(1)} %bitcast.174, f32[1024]{0:T(1024)S(1)} %bitcast.172, f32[2048]{0:T(1024)S(1)} %get-tuple-element.64, f32[2048]{0:T(1024)S(1)} %fusion.311, ...), kind=kOutput, calls=%fused_computation.114 | convolution fusion | flops 2044723200 | bytes 9408512 | tf_op jit(solution)/shard_map/dot_general | solution.py:87
  242.7 3.5 collective-permute-start.2
  246.2 6.9 %fusion.371 = f32[1024,2048]{1,0:T(8,128)S(1)} fusion(f32[80,1024]{1,0:T(8,128)S(1)} %collective-permute-done.3, f32[80,2048]{1,0:T(8,128)S(1)} %reshape.255), kind=kOutput, calls=%fused_computation.411 | convolution fusion | flops 2013265920 | bytes 9371648 | tf_op jit(solution)/shard_map/dot_general | solution.py:70
  253.8 9.8 %fusion.269 = f32[80,2048]{1,0:T(8,128)S(1)} fusion(f32[80,2048]{1,0:T(8,128)S(1)} %fusion.80, f32[80,2048]{1,0:T(8,128)S(1)} %fusion.96, f32[80,2048]{1,0:T(8,128)S(1)} %fusion.112, f32[80,2048]{1,0:T(8,128)S(1)} %fusion.144, f32[80,1024]{1,0:T(8,128)S(1)} %collective-permute-done.2, f32[1024,2048]{1,0:T(8,128)S(1)} %fusion.371, f32[1024]{0:T(1024)S(1)} %bitcast.164, ...), kind=kOutput, calls=%fused_computation.265 | convolution fusion | flops 2045378560 | bytes 12029952 | tf_op jit(solution)/shard_map/dot_general | solution.py:87
  265.1 3.5 all-to-all-start.2
  269.3 11.0 %all-to-all-done.2 = f32[80,2,4,256]{3,2,1,0:T(4,128)S(1)} async-done(((f32[80,2,4,256]{3,2,1,0:T(4,128)}), f32[80,2,4,256]{3,2,1,0:T(4,128)S(1)}, u32[]{:S(2)}, u32[]{:S(2)}) %all-to-all-start.2) | async-done | bytes 655392 | tf_op jit(solution)/shard_map/all_to_all | solution.py:182
  280.3 4.7 copy.140
  285.0 6.2 %gather_fusion.1 = f32[1024,10]{1,0:T(8,128)S(1)} fusion(f32[10,16384]{0,1:T(8,128)} %bitcast.114, s32[1024]{0:T(1024)S(1)} %fusion.317), kind=kCustom, calls=%fused_computation.1.clone | custom fusion | bytes 86016 | tf_op jit(solution)/shard_map/jit(_take)/gather | solution.py:160
  292.4 3.5 all-to-all-start.4
  296.5 12.0 %copy.141 = f32[10,2,4,8,256]{0,2,1,4,3:T(4,128)} copy(f32[10,2,4,8,256]{0,4,3,2,1:T(8,128)} %bitcast.115) | data formatting | bytes 1310720 | tf_op jit(solution)/shard_map/all_to_all | solution.py:182
  308.6 12.2 %reshape.285 = f32[8,1,20480]{2,1,0:T(1,128)} reshape(f32[2048,2,4,10]{3,2,1,0:T(4,128)} %bitcast.118) | data formatting | bytes 1310720
  320.8 4.7 all-to-all-start.3
  325.9 3.9 collective-permute-start.23
  329.8 2.8 collective-permute-start.20
  332.6 6.0 %collective-permute-start.24 = (f32[80,1024]{1,0:T(8,128)S(1)}, f32[80,1024]{1,0:T(8,128)S(1)}, u32[]{:S(2)}, u32[]{:S(2)}) collective-permute-start(f32[80,1024]{1,0:T(8,128)S(1)} %get-tuple-element.8), channel_id=1, source_target_pairs={{16,0},{24,8},{32,16},{40,24},{48,32},{56,40},{64,48},{72,56},{80,... | collective-permute-start | bytes 983048 | tf_op jit(solution)/shard_map/ppermute | solution.py:33
  340.6 7.4 %collective-permute-start.17 = (f32[80,1024]{1,0:T(8,128)S(1)}, f32[80,1024]{1,0:T(8,128)}, u32[]{:S(2)}, u32[]{:S(2)}) collective-permute-start(f32[80,1024]{1,0:T(8,128)S(1)} %get-tuple-element.9), channel_id=1, source_target_pairs={{8,0},{16,8},{24,16},{32,24},{40,32},{48,40},{56,48},{64,56},{72,6... | collective-permute-start | bytes 983048 | tf_op jit(solution)/shard_map/ppermute | solution.py:33
  348.2 2.2 reduce.5
  350.4 14.6 %reshape.286 = f32[2048,2,4,10]{3,2,1,0:T(4,128)} reshape(f32[8,20480]{1,0:T(8,128)S(1)} %reduce.5) | data formatting | bytes 1310720
  365.0 5.7 %copy.148 = f32[10,2,4,8,256]{4,3,2,1,0:T(8,128)S(1)} copy(f32[10,2,4,8,256]{0,2,1,4,3:T(4,128)} %bitcast.119) | data formatting | bytes 1310720 | tf_op jit(solution)/shard_map/all_to_all | solution.py:164
  371.3 6.9 %fusion.375 = f32[1024,2048]{1,0:T(8,128)S(1)} fusion(f32[80,1024]{1,0:T(8,128)S(1)} %div.220, f32[80,2048]{1,0:T(8,128)S(1)} %reshape.259), kind=kOutput, calls=%fused_computation.415 | convolution fusion | flops 2013265920 | bytes 9371648 | tf_op jit(solution)/shard_map/dot_general | solution.py:70
  378.3 9.7 %fusion.64 = f32[80,2048]{1,0:T(8,128)S(1)} fusion(f32[80,1024]{1,0:T(8,128)S(1)} %get-tuple-element.9, f32[1024,2048]{1,0:T(8,128)S(1)} %fusion.375, f32[1024]{0:T(1024)S(1)} %bitcast.146, f32[1024]{0:T(1024)S(1)} %bitcast.147, f32[1024]{0:T(1024)S(1)} %bitcast.145, f32[2048]{0:T(1024)S(1)} %get-tuple-element.64, f32[2048]{0:T(1024)S(1)} %fusion.311, ...), kind=kOutput, calls=%fused_computation.66 | convolution fusion | flops 2044723200 | bytes 9408512 | tf_op jit(solution)/shard_map/dot_general | solution.py:87
  390.2 6.9 %fusion.379 = f32[1024,2048]{1,0:T(8,128)S(1)} fusion(f32[80,1024]{1,0:T(8,128)S(1)} %collective-permute-done.24, f32[80,2048]{1,0:T(8,128)S(1)} %reshape.259), kind=kOutput, calls=%fused_computation.419 | convolution fusion | flops 2013265920 | bytes 9371648 | tf_op jit(solution)/shard_map/dot_general | solution.py:70
  397.2 3.9 collective-permute-start.14
  401.0 10.5 %fusion = f32[80,2048]{1,0:T(8,128)S(1)} fusion(f32[80,1024]{1,0:T(8,128)} %collective-permute-done.23, f32[1024,2048]{1,0:T(8,128)S(1)} %fusion.379, f32[1024]{0:T(1024)S(1)} %bitcast.167, f32[1024]{0:T(1024)S(1)} %bitcast.168, f32[1024]{0:T(1024)S(1)} %bitcast.166, f32[2048]{0:T(1024)S(1)} %get-tuple-element.64, f32[2048]{0:T(1024)S(1)} %fusion.311, ...), kind=kOutput, calls=%fused_computation.2 | convolution fusion | flops 2044723200 | bytes 9408512 | tf_op jit(solution)/shard_map/dot_general | solution.py:87
  411.6 2.3 collective-permute-start.15
  413.9 6.9 %fusion.378 = f32[1024,2048]{1,0:T(8,128)S(1)} fusion(f32[80,1024]{1,0:T(8,128)S(1)} %collective-permute-done.21, f32[80,2048]{1,0:T(8,128)S(1)} %reshape.259), kind=kOutput, calls=%fused_computation.418 | convolution fusion | flops 2013265920 | bytes 9371648 | tf_op jit(solution)/shard_map/dot_general | solution.py:70
  420.9 10.7 %fusion.16 = f32[80,2048]{1,0:T(8,128)S(1)} fusion(f32[80,1024]{1,0:T(8,128)} %collective-permute-done.20, f32[1024,2048]{1,0:T(8,128)S(1)} %fusion.378, f32[1024]{0:T(1024)S(1)} %bitcast.158, f32[1024]{0:T(1024)S(1)} %bitcast.159, f32[1024]{0:T(1024)S(1)} %bitcast.157, f32[2048]{0:T(1024)S(1)} %get-tuple-element.64, f32[2048]{0:T(1024)S(1)} %fusion.311, ...), kind=kOutput, calls=%fused_computation.18 | convolution fusion | flops 2044723200 | bytes 9408512 | tf_op jit(solution)/shard_map/dot_general | solution.py:87
  431.6 6.9 %fusion.377 = f32[1024,2048]{1,0:T(8,128)S(1)} fusion(f32[80,1024]{1,0:T(8,128)S(1)} %collective-permute-done.18, f32[80,2048]{1,0:T(8,128)S(1)} %reshape.259), kind=kOutput, calls=%fused_computation.417 | convolution fusion | flops 2013265920 | bytes 9371648 | tf_op jit(solution)/shard_map/dot_general | solution.py:70
  438.5 10.7 %fusion.32 = f32[80,2048]{1,0:T(8,128)S(1)} fusion(f32[80,1024]{1,0:T(8,128)} %collective-permute-done.17, f32[1024,2048]{1,0:T(8,128)S(1)} %fusion.377, f32[1024]{0:T(1024)S(1)} %bitcast.170, f32[1024]{0:T(1024)S(1)} %bitcast.171, f32[1024]{0:T(1024)S(1)} %bitcast.169, f32[2048]{0:T(1024)S(1)} %get-tuple-element.64, f32[2048]{0:T(1024)S(1)} %fusion.311, ...), kind=kOutput, calls=%fused_computation.34 | convolution fusion | flops 2044723200 | bytes 9408512 | tf_op jit(solution)/shard_map/dot_general | solution.py:87
  449.3 7.2 %fusion.376 = f32[1024,2048]{1,0:T(8,128)S(1)} fusion(f32[80,1024]{1,0:T(8,128)S(1)} %collective-permute-done.15, f32[80,2048]{1,0:T(8,128)S(1)} %reshape.259), kind=kOutput, calls=%fused_computation.416 | convolution fusion | flops 2013265920 | bytes 9371648 | tf_op jit(solution)/shard_map/dot_general | solution.py:70
  456.5 9.6 %fusion.281 = f32[80,2048]{1,0:T(8,128)S(1)} fusion(f32[80,2048]{1,0:T(8,128)S(1)} %fusion, f32[80,2048]{1,0:T(8,128)S(1)} %fusion.16, f32[80,2048]{1,0:T(8,128)S(1)} %fusion.32, f32[80,2048]{1,0:T(8,128)S(1)} %fusion.64, f32[80,1024]{1,0:T(8,128)S(1)} %collective-permute-done.14, f32[1024,2048]{1,0:T(8,128)S(1)} %fusion.376, f32[1024]{0:T(1024)S(1)} %bitcast.161, ...), kind=kOutput, calls=%fused_computation.269 | convolution fusion | flops 2045378560 | bytes 12029952 | tf_op jit(solution)/shard_map/dot_general | solution.py:87
  466.8 16.4 %all_to_all.82 = f32[80,2,4,256]{3,2,1,0:T(4,128)S(1)} all-to-all(f32[80,2,4,256]{3,2,1,0:T(4,128)S(1)} %bitcast_add_fusion.1), channel_id=1, replica_groups=mesh['tile'=32,'ens'=8] {'ens'}, dimensions={0} | all-to-all | bytes 1310720 | tf_op jit(solution)/shard_map/all_to_all | solution.py:182
  (102 shorter events, 37.4 us)
Async XLA Ops:
  0.9 30.5 %collective-permute-start.13 = (f32[3,1024]{1,0:T(4,128)S(1)}, f32[3,1024]{1,0:T(4,128)S(1)}, u32[]{:S(2)}, u32[]{:S(2)}) collective-permute-start(f32[3,1024]{1,0:T(4,128)S(1)} %bitcast.139), channel_id=1, source_target_pairs={{16,0},{24,8},{32,16},{40,24},{48,32},{56,40},{64,48},{72,56},{80,... | collective-permute-start | bytes 36872 | tf_op jit(solution)/shard_map/ppermute | solution.py:33
  9.3 24.0 %collective-permute-start.10 = (f32[3,1024]{1,0:T(4,128)S(1)}, f32[3,1024]{1,0:T(4,128)S(1)}, u32[]{:S(2)}, u32[]{:S(2)}) collective-permute-start(f32[3,1024]{1,0:T(4,128)S(1)} %bitcast.140), channel_id=1, source_target_pairs={{0,16},{8,24},{16,32},{24,40},{32,48},{40,56},{48,64},{56,72},{64,... | collective-permute-start | bytes 36872 | tf_op jit(solution)/shard_map/ppermute | solution.py:33
  11.3 59.6 %collective-permute-start.7 = (f32[3,1024]{1,0:T(4,128)S(1)}, f32[3,1024]{1,0:T(4,128)S(1)}, u32[]{:S(2)}, u32[]{:S(2)}) collective-permute-start(f32[3,1024]{1,0:T(4,128)S(1)} %bitcast.141), channel_id=1, source_target_pairs={{8,0},{16,8},{24,16},{32,24},{40,32},{48,40},{56,48},{64,56},{72,6... | collective-permute-start | bytes 36872 | tf_op jit(solution)/shard_map/ppermute | solution.py:33
  17.8 55.1 %collective-permute-start.4 = (f32[3,1024]{1,0:T(4,128)S(1)}, f32[3,1024]{1,0:T(4,128)S(1)}, u32[]{:S(2)}, u32[]{:S(2)}) collective-permute-start(f32[3,1024]{1,0:T(4,128)S(1)} %bitcast.142), channel_id=1, source_target_pairs={{0,8},{8,16},{16,24},{24,32},{32,40},{40,48},{48,56},{56,64},{64,7... | collective-permute-start | bytes 36872 | tf_op jit(solution)/shard_map/ppermute | solution.py:33
  21.4 15.3 %collective-permute-start.1 = (f32[10,2,1,2048]{3,0,2,1:T(8,128)S(1)}, f32[10,2,1,2048]{3,0,2,1:T(8,128)S(1)}, u32[]{:S(2)}, u32[]{:S(2)}) collective-permute-start(f32[10,2,1,2048]{3,0,2,1:T(8,128)S(1)} %copy.152), channel_id=1, source_target_pairs={{8,0},{16,8},{24,16},{32,24},{40,32},{48,40},{56,48},{64,56},{72,6... | collective-permute-start | bytes 491528 | tf_op jit(solution)/shard_map/ppermute | solution.py:23
  31.4 10.6 %collective-permute-start = (f32[10,2,1,2048]{3,0,2,1:T(8,128)S(1)}, f32[10,2,1,2048]{3,0,2,1:T(8,128)S(1)}, u32[]{:S(2)}, u32[]{:S(2)}) collective-permute-start(f32[10,2,1,2048]{3,0,2,1:T(8,128)S(1)} %copy.151), channel_id=1, source_target_pairs={{0,8},{8,16},{16,24},{24,32},{32,40},{40,48},{48,56},{56,64},{64,7... | collective-permute-start | bytes 491528 | tf_op jit(solution)/shard_map/ppermute | solution.py:21
  33.3 235.9 %collective-permute-start.25 = (f32[3,1024]{1,0:T(4,128)S(1)}, f32[3,1024]{1,0:T(4,128)S(1)}, u32[]{:S(2)}, u32[]{:S(2)}) collective-permute-start(f32[3,1024]{1,0:T(4,128)S(1)} %bitcast.135), channel_id=1, source_target_pairs={{16,0},{24,8},{32,16},{40,24},{48,32},{56,40},{64,48},{72,56},{80,... | collective-permute-start | bytes 36872 | tf_op jit(solution)/shard_map/ppermute | solution.py:33
  36.8 232.5 %collective-permute-start.22 = (f32[3,1024]{1,0:T(4,128)S(1)}, f32[3,1024]{1,0:T(4,128)S(1)}, u32[]{:S(2)}, u32[]{:S(2)}) collective-permute-start(f32[3,1024]{1,0:T(4,128)S(1)} %bitcast.136), channel_id=1, source_target_pairs={{0,16},{8,24},{16,32},{24,40},{32,48},{40,56},{48,64},{56,72},{64,... | collective-permute-start | bytes 36872 | tf_op jit(solution)/shard_map/ppermute | solution.py:33
  42.0 253.9 %collective-permute-start.19 = (f32[3,1024]{1,0:T(4,128)S(1)}, f32[3,1024]{1,0:T(4,128)S(1)}, u32[]{:S(2)}, u32[]{:S(2)}) collective-permute-start(f32[3,1024]{1,0:T(4,128)S(1)} %bitcast.137), channel_id=1, source_target_pairs={{8,0},{16,8},{24,16},{32,24},{40,32},{48,40},{56,48},{64,56},{72,6... | collective-permute-start | bytes 36872 | tf_op jit(solution)/shard_map/ppermute | solution.py:33
  66.4 24.8 %all-to-all-start.1 = ((f32[8,10,1024]{2,1,0:T(8,128)}), f32[8,10,1024]{2,1,0:T(8,128)S(1)}, u32[]{:S(2)}, u32[]{:S(2)}) async-start(f32[8,10,1024]{2,1,0:T(8,128)} %stack.4), calls=%async_computation.1 | async-start | bytes 1048576 | tf_op jit(solution)/shard_map/all_to_all | solution.py:162
  70.9 225.6 %collective-permute-start.16 = (f32[3,1024]{1,0:T(4,128)S(1)}, f32[3,1024]{1,0:T(4,128)S(1)}, u32[]{:S(2)}, u32[]{:S(2)}) collective-permute-start(f32[3,1024]{1,0:T(4,128)S(1)} %bitcast.138), channel_id=1, source_target_pairs={{0,8},{8,16},{16,24},{24,32},{32,40},{40,48},{48,56},{56,64},{64,7... | collective-permute-start | bytes 36872 | tf_op jit(solution)/shard_map/ppermute | solution.py:33
  72.9 23.3 %copy-start = (f32[2,1024]{1,0:T(2,128)S(1)}, f32[2,1024]{1,0:T(2,128)}, u32[]{:S(2)}) copy-start(f32[2,1024]{1,0:T(2,128)} %param.13) | copy-start | bytes 24580
  72.9 23.3 %copy-start.1 = (f32[2,1024]{1,0:T(2,128)S(1)}, f32[2,1024]{1,0:T(2,128)}, u32[]{:S(2)}) copy-start(f32[2,1024]{1,0:T(2,128)} %param.12) | copy-start | bytes 24580
  91.2 16.5 %all-to-all-start = ((f32[8,1,20480]{2,1,0:T(1,128)}), f32[8,1,20480]{2,1,0:T(1,128)S(1)}, u32[]{:S(2)}, u32[]{:S(2)}) async-start(f32[8,1,20480]{2,1,0:T(1,128)} %reshape.283), calls=%async_computation | async-start | bytes 1310720 | tf_op jit(solution)/shard_map/all_to_all | solution.py:164
  96.3 53.0 %collective-permute-start.12 = (f32[80,1024]{1,0:T(8,128)S(1)}, f32[80,1024]{1,0:T(8,128)S(1)}, u32[]{:S(2)}, u32[]{:S(2)}) collective-permute-start(f32[80,1024]{1,0:T(8,128)S(1)} %get-tuple-element.10), channel_id=1, source_target_pairs={{16,0},{24,8},{32,16},{40,24},{48,32},{56,40},{64,48},{72,56},{80,... | collective-permute-start | bytes 983048 | tf_op jit(solution)/shard_map/ppermute | solution.py:33
  149.4 17.3 %collective-permute-start.11 = (f32[80,1024]{1,0:T(8,128)S(1)}, f32[80,1024]{1,0:T(8,128)S(1)}, u32[]{:S(2)}, u32[]{:S(2)}) collective-permute-start(f32[80,1024]{1,0:T(8,128)S(1)} %get-tuple-element.11), channel_id=1, source_target_pairs={{16,0},{24,8},{32,16},{40,24},{48,32},{56,40},{64,48},{72,56},{80,... | collective-permute-start | bytes 983048 | tf_op jit(solution)/shard_map/ppermute | solution.py:33
  166.7 21.5 %collective-permute-start.9 = (f32[80,1024]{1,0:T(8,128)S(1)}, f32[80,1024]{1,0:T(8,128)S(1)}, u32[]{:S(2)}, u32[]{:S(2)}) collective-permute-start(f32[80,1024]{1,0:T(8,128)S(1)} %get-tuple-element.10), channel_id=1, source_target_pairs={{0,16},{8,24},{16,32},{24,40},{32,48},{40,56},{48,64},{56,72},{64,... | collective-permute-start | bytes 983048 | tf_op jit(solution)/shard_map/ppermute | solution.py:33
  188.2 19.0 %collective-permute-start.8 = (f32[80,1024]{1,0:T(8,128)S(1)}, f32[80,1024]{1,0:T(8,128)S(1)}, u32[]{:S(2)}, u32[]{:S(2)}) collective-permute-start(f32[80,1024]{1,0:T(8,128)S(1)} %get-tuple-element.11), channel_id=1, source_target_pairs={{0,16},{8,24},{16,32},{24,40},{32,48},{40,56},{48,64},{56,72},{64,... | collective-permute-start | bytes 983048 | tf_op jit(solution)/shard_map/ppermute | solution.py:33
  207.2 11.9 %collective-permute-start.6 = (f32[80,1024]{1,0:T(8,128)S(1)}, f32[80,1024]{1,0:T(8,128)S(1)}, u32[]{:S(2)}, u32[]{:S(2)}) collective-permute-start(f32[80,1024]{1,0:T(8,128)S(1)} %get-tuple-element.10), channel_id=1, source_target_pairs={{8,0},{16,8},{24,16},{32,24},{40,32},{48,40},{56,48},{64,56},{72,6... | collective-permute-start | bytes 983048 | tf_op jit(solution)/shard_map/ppermute | solution.py:33
  219.2 10.2 %collective-permute-start.5 = (f32[80,1024]{1,0:T(8,128)S(1)}, f32[80,1024]{1,0:T(8,128)S(1)}, u32[]{:S(2)}, u32[]{:S(2)}) collective-permute-start(f32[80,1024]{1,0:T(8,128)S(1)} %get-tuple-element.11), channel_id=1, source_target_pairs={{8,0},{16,8},{24,16},{32,24},{40,32},{48,40},{56,48},{64,56},{72,6... | collective-permute-start | bytes 983048 | tf_op jit(solution)/shard_map/ppermute | solution.py:33
  229.3 13.4 %collective-permute-start.3 = (f32[80,1024]{1,0:T(8,128)S(1)}, f32[80,1024]{1,0:T(8,128)S(1)}, u32[]{:S(2)}, u32[]{:S(2)}) collective-permute-start(f32[80,1024]{1,0:T(8,128)S(1)} %get-tuple-element.10), channel_id=1, source_target_pairs={{0,8},{8,16},{16,24},{24,32},{32,40},{40,48},{48,56},{56,64},{64,7... | collective-permute-start | bytes 983048 | tf_op jit(solution)/shard_map/ppermute | solution.py:33
  242.7 11.1 %collective-permute-start.2 = (f32[80,1024]{1,0:T(8,128)S(1)}, f32[80,1024]{1,0:T(8,128)S(1)}, u32[]{:S(2)}, u32[]{:S(2)}) collective-permute-start(f32[80,1024]{1,0:T(8,128)S(1)} %get-tuple-element.11), channel_id=1, source_target_pairs={{0,8},{8,16},{16,24},{24,32},{32,40},{40,48},{48,56},{56,64},{64,7... | collective-permute-start | bytes 983048 | tf_op jit(solution)/shard_map/ppermute | solution.py:33
  265.1 15.2 %all-to-all-start.2 = ((f32[80,2,4,256]{3,2,1,0:T(4,128)}), f32[80,2,4,256]{3,2,1,0:T(4,128)S(1)}, u32[]{:S(2)}, u32[]{:S(2)}) async-start(f32[80,2,4,256]{3,2,1,0:T(4,128)} %bitcast_add_fusion), calls=%async_computation.2 | async-start | bytes 1310720 | tf_op jit(solution)/shard_map/all_to_all | solution.py:182
  292.4 28.4 %all-to-all-start.4 = ((f32[8,10,1024]{2,1,0:T(8,128)}), f32[8,10,1024]{2,1,0:T(8,128)S(1)}, u32[]{:S(2)}, u32[]{:S(2)}) async-start(f32[8,10,1024]{2,1,0:T(8,128)} %stack.5), calls=%async_computation.4 | async-start | bytes 1048576 | tf_op jit(solution)/shard_map/all_to_all | solution.py:162
  320.8 27.4 %all-to-all-start.3 = ((f32[8,1,20480]{2,1,0:T(1,128)}), f32[8,1,20480]{2,1,0:T(1,128)S(1)}, u32[]{:S(2)}, u32[]{:S(2)}) async-start(f32[8,1,20480]{2,1,0:T(1,128)} %reshape.285), calls=%async_computation.3 | async-start | bytes 1310720 | tf_op jit(solution)/shard_map/all_to_all | solution.py:164
  325.9 71.3 %collective-permute-start.23 = (f32[80,1024]{1,0:T(8,128)S(1)}, f32[80,1024]{1,0:T(8,128)}, u32[]{:S(2)}, u32[]{:S(2)}) collective-permute-start(f32[80,1024]{1,0:T(8,128)S(1)} %get-tuple-element.9), channel_id=1, source_target_pairs={{16,0},{24,8},{32,16},{40,24},{48,32},{56,40},{64,48},{72,56},{80,... | collective-permute-start | bytes 983048 | tf_op jit(solution)/shard_map/ppermute | solution.py:33
  329.8 91.0 %collective-permute-start.20 = (f32[80,1024]{1,0:T(8,128)S(1)}, f32[80,1024]{1,0:T(8,128)}, u32[]{:S(2)}, u32[]{:S(2)}) collective-permute-start(f32[80,1024]{1,0:T(8,128)S(1)} %get-tuple-element.9), channel_id=1, source_target_pairs={{0,16},{8,24},{16,32},{24,40},{32,48},{40,56},{48,64},{56,72},{64,... | collective-permute-start | bytes 983048 | tf_op jit(solution)/shard_map/ppermute | solution.py:33
  332.6 55.4 %collective-permute-start.24 = (f32[80,1024]{1,0:T(8,128)S(1)}, f32[80,1024]{1,0:T(8,128)S(1)}, u32[]{:S(2)}, u32[]{:S(2)}) collective-permute-start(f32[80,1024]{1,0:T(8,128)S(1)} %get-tuple-element.8), channel_id=1, source_target_pairs={{16,0},{24,8},{32,16},{40,24},{48,32},{56,40},{64,48},{72,56},{80,... | collective-permute-start | bytes 983048 | tf_op jit(solution)/shard_map/ppermute | solution.py:33
  338.7 72.9 %collective-permute-start.21 = (f32[80,1024]{1,0:T(8,128)S(1)}, f32[80,1024]{1,0:T(8,128)S(1)}, u32[]{:S(2)}, u32[]{:S(2)}) collective-permute-start(f32[80,1024]{1,0:T(8,128)S(1)} %get-tuple-element.8), channel_id=1, source_target_pairs={{0,16},{8,24},{16,32},{24,40},{32,48},{40,56},{48,64},{56,72},{64,... | collective-permute-start | bytes 983048 | tf_op jit(solution)/shard_map/ppermute | solution.py:33
  340.6 97.9 %collective-permute-start.17 = (f32[80,1024]{1,0:T(8,128)S(1)}, f32[80,1024]{1,0:T(8,128)}, u32[]{:S(2)}, u32[]{:S(2)}) collective-permute-start(f32[80,1024]{1,0:T(8,128)S(1)} %get-tuple-element.9), channel_id=1, source_target_pairs={{8,0},{16,8},{24,16},{32,24},{40,32},{48,40},{56,48},{64,56},{72,6... | collective-permute-start | bytes 983048 | tf_op jit(solution)/shard_map/ppermute | solution.py:33
  388.0 43.6 %collective-permute-start.18 = (f32[80,1024]{1,0:T(8,128)S(1)}, f32[80,1024]{1,0:T(8,128)S(1)}, u32[]{:S(2)}, u32[]{:S(2)}) collective-permute-start(f32[80,1024]{1,0:T(8,128)S(1)} %get-tuple-element.8), channel_id=1, source_target_pairs={{8,0},{16,8},{24,16},{32,24},{40,32},{48,40},{56,48},{64,56},{72,6... | collective-permute-start | bytes 983048 | tf_op jit(solution)/shard_map/ppermute | solution.py:33
  397.2 59.3 %collective-permute-start.14 = (f32[80,1024]{1,0:T(8,128)S(1)}, f32[80,1024]{1,0:T(8,128)S(1)}, u32[]{:S(2)}, u32[]{:S(2)}) collective-permute-start(f32[80,1024]{1,0:T(8,128)S(1)} %get-tuple-element.9), channel_id=1, source_target_pairs={{0,8},{8,16},{16,24},{24,32},{32,40},{40,48},{48,56},{56,64},{64,7... | collective-permute-start | bytes 983048 | tf_op jit(solution)/shard_map/ppermute | solution.py:33
  411.6 37.7 %collective-permute-start.15 = (f32[80,1024]{1,0:T(8,128)S(1)}, f32[80,1024]{1,0:T(8,128)S(1)}, u32[]{:S(2)}, u32[]{:S(2)}) collective-permute-start(f32[80,1024]{1,0:T(8,128)S(1)} %get-tuple-element.8), channel_id=1, source_target_pairs={{0,8},{8,16},{16,24},{24,32},{32,40},{40,48},{48,56},{56,64},{64,7... | collective-permute-start | bytes 983048 | tf_op jit(solution)/shard_map/ppermute | solution.py:33
  431.5 7.0 %copy-start.2 = (f32[1,1024]{1,0:T(1,128)S(1)}, f32[1,1024]{1,0:T(1,128)}, u32[]{:S(2)}) copy-start(f32[1,1024]{1,0:T(1,128)} %get-tuple-element.25) | copy-start | bytes 12292
